TPU v7x, 32 devices: a whole 2x2x4 slice. The times are simulated.
32 devices in a mesh: fsdp: 4 (over y, core), ctx: 4 (over z), tp: 2 (over x).
Axes of the slice: x: 2, y: 2, z: 4, core: 2. Of those that a mesh axis runs over, the one named last changes fastest.
Arguments:
- layer_input: bfloat16 [4, 1024, 1536], P('fsdp', 'ctx'), may hold values from -6 to 6
- segments: int32 [4, 1024], P('fsdp', 'ctx'), may hold values from 0 to 5, as said below
- positions: int32 [4, 1024], P('fsdp', 'ctx'), may hold values from 0 to 1023, as said below
- attn_gain: bfloat16 [1536], P(('fsdp', 'ctx')), may hold values from 0.099609375 to 1.8984375
- query_proj: bfloat16 [1536, 1536], P(('fsdp', 'ctx'), 'tp'), may hold values from -0.21875 to 0.21875
- key_proj: bfloat16 [1536, 768], P(('fsdp', 'ctx'), 'tp'), may hold values from -0.21875 to 0.21875
- value_proj: bfloat16 [1536, 768], P(('fsdp', 'ctx'), 'tp'), may hold values from -0.15625 to 0.15625
- out_proj: bfloat16 [1536, 1536], P('tp', ('fsdp', 'ctx')), may hold values from -1.25 to 1.25
- mlp_gain: bfloat16 [1536], P(('fsdp', 'ctx')), may hold values from 0.099609375 to 1.8984375
- gate_proj: bfloat16 [1536, 4096], P(('fsdp', 'ctx'), 'tp'), may hold values from -0.15625 to 0.15625
- up_proj: bfloat16 [1536, 4096], P(('fsdp', 'ctx'), 'tp'), may hold values from -0.15625 to 0.15625
- down_proj: bfloat16 [4096, 1536], P('tp', ('fsdp', 'ctx')), may hold values from -0.09375 to 0.09375
- out_grad: bfloat16 [4, 1024, 1536], P('fsdp', 'ctx'), may hold values from -6 to 6
Outputs:
- layer_output: bfloat16 [4, 1024, 1536], P('fsdp', 'ctx')
- input_grad: bfloat16 [4, 1024, 1536], P('fsdp', 'ctx')
- attn_gain_grad: float32 [1536], P(('fsdp', 'ctx'))
- query_proj_grad: float32 [1536, 1536], P(('fsdp', 'ctx'), 'tp')
- key_proj_grad: float32 [1536, 768], P(('fsdp', 'ctx'), 'tp')
- value_proj_grad: float32 [1536, 768], P(('fsdp', 'ctx'), 'tp')
- out_proj_grad: float32 [1536, 1536], P('tp', ('fsdp', 'ctx'))
- mlp_gain_grad: float32 [1536], P(('fsdp', 'ctx'))
- gate_proj_grad: float32 [1536, 4096], P(('fsdp', 'ctx'), 'tp')
- up_proj_grad: float32 [1536, 4096], P(('fsdp', 'ctx'), 'tp')
- down_proj_grad: float32 [4096, 1536], P('tp', ('fsdp', 'ctx'))
Inputs may be any that keep to these rules, and one draw needn't show every extreme that they name: `segments`: numbers the documents of each sequence 0, 1, 2 and so on, never falling; every document has 200 to 2000 tokens except that the last of a sequence may be cut short. `positions`: each token's offset from the first token of its document.
All inputs are finite; a program needn't handle non-finite values.
Results may differ from a plain program's by a relative error of at most 0.018.
Values may be sent and summed in bfloat16 or wider, within the bound.
A program may use at most 192 MiB of HBM per device.

v0:
```python
import jax
import jax.numpy as jnp
from jax import lax
from jax.sharding import PartitionSpec as P

HQ = 16
HK = 8
DH = 96
EPS = 1e-05
THETA = 100000.0
NEGATIVE = -1e30


def rotary_tables(positions):
    half_dim = DH // 2
    freq_index = jnp.arange(half_dim, dtype=jnp.float32)
    inverse = THETA ** (-2.0 * freq_index / DH)
    angles = positions.astype(jnp.float32)[..., None] * inverse
    return (jnp.cos(angles), jnp.sin(angles))


def rotate(field_in, cos_table, sin_table):
    half_dim = field_in.shape[-1] // 2
    front_half = field_in[..., :half_dim]
    back_half = field_in[..., half_dim:]
    return jnp.concatenate(
        [
            front_half * cos_table - back_half * sin_table,
            back_half * cos_table + front_half * sin_table,
        ],
        axis=-1,
    )


def unrotate(field_in, cos_table, sin_table):
    half_dim = field_in.shape[-1] // 2
    front_half = field_in[..., :half_dim]
    back_half = field_in[..., half_dim:]
    return jnp.concatenate(
        [
            front_half * cos_table + back_half * sin_table,
            back_half * cos_table - front_half * sin_table,
        ],
        axis=-1,
    )


def inverse_rms(values):
    return lax.rsqrt(jnp.mean(values * values, axis=-1, keepdims=True) + EPS)


def contract(left, right, left_dim, right_dim):
    return lax.dot_general(
        left, right, (((left_dim,), (right_dim,)), ((), ())), preferred_element_type=jnp.float32
    )


def norm_back(upstream, inner, values, scale_rows):
    cubed = scale_rows * scale_rows * scale_rows
    return (
        upstream
        + scale_rows * inner
        - values * cubed * jnp.mean(inner * values, axis=-1, keepdims=True)
    )


def to_blocks(matrix, seq_count, local_kv, groups):
    span = matrix.shape[0] // seq_count
    shaped = matrix.reshape(seq_count, span, local_kv, groups, DH).transpose(0, 2, 1, 3, 4)
    return shaped.reshape(seq_count * local_kv, span * groups, DH)


def from_blocks(blocks, seq_count, local_kv, groups):
    span = blocks.shape[1] // groups
    shaped = blocks.reshape(seq_count, local_kv, span, groups, DH).transpose(0, 2, 1, 3, 4)
    return shaped.reshape(seq_count * span, local_kv * groups * DH)


def seq_items(matrix, local_kv):
    seq_count = matrix.shape[0]
    length = matrix.shape[1]
    return (
        matrix.reshape(seq_count, length, local_kv, DH)
        .transpose(0, 2, 1, 3)
        .reshape(seq_count * local_kv, length, DH)
    )


def from_items(items, seq_count, local_kv):
    length = items.shape[1]
    return (
        items.reshape(seq_count, local_kv, length, DH)
        .transpose(0, 2, 1, 3)
        .reshape(seq_count, length, local_kv * DH)
    )


def on_device(
    layer_input,
    segments,
    positions,
    attn_gain,
    query_proj,
    key_proj,
    value_proj,
    out_proj,
    mlp_gain,
    gate_proj,
    up_proj,
    down_proj,
    out_grad,
):
    attn_full = (
        lax.all_gather(attn_gain, ("fsdp", "ctx"), axis=0, tiled=True),
        lax.all_gather(query_proj, ("fsdp", "ctx"), axis=0, tiled=True),
        lax.all_gather(key_proj, ("fsdp", "ctx"), axis=0, tiled=True),
        lax.all_gather(value_proj, ("fsdp", "ctx"), axis=0, tiled=True),
        lax.all_gather(out_proj, ("fsdp", "ctx"), axis=1, tiled=True),
    )
    mlp_full = (
        lax.all_gather(mlp_gain, ("fsdp", "ctx"), axis=0, tiled=True),
        lax.all_gather(gate_proj, ("fsdp", "ctx"), axis=0, tiled=True),
        lax.all_gather(up_proj, ("fsdp", "ctx"), axis=0, tiled=True),
        lax.all_gather(down_proj, ("fsdp", "ctx"), axis=1, tiled=True),
    )
    seq_count, span, width = layer_input.shape
    total_rows = seq_count * span
    groups = HQ // HK
    local_kv = key_proj.shape[1] // DH
    score_scale = DH ** (-0.5)
    inputs = layer_input.reshape(total_rows, width).astype(jnp.float32)
    scale_attn = inverse_rms(inputs)
    normed_attn = (inputs * scale_attn * attn_full[0].astype(jnp.float32)).astype(jnp.bfloat16)
    query_pre = jnp.dot(normed_attn, attn_full[1], preferred_element_type=jnp.float32)
    key_pre = jnp.dot(normed_attn, attn_full[2], preferred_element_type=jnp.float32)
    value_pre = jnp.dot(normed_attn, attn_full[3], preferred_element_type=jnp.float32)
    cos_table, sin_table = rotary_tables(positions.reshape(total_rows))
    cos_table = cos_table[:, None, :]
    sin_table = sin_table[:, None, :]
    query_rot = (
        rotate(query_pre.reshape(total_rows, -1, DH), cos_table, sin_table)
        .astype(jnp.bfloat16)
        .reshape(total_rows, -1)
    )
    key_rot = (
        rotate(key_pre.reshape(total_rows, local_kv, DH), cos_table, sin_table)
        .astype(jnp.bfloat16)
        .reshape(seq_count, span, local_kv * DH)
    )
    value_low = value_pre.astype(jnp.bfloat16).reshape(seq_count, span, local_kv * DH)
    key_all, value_all, segment_all = (
        lax.all_gather(key_rot, "ctx", axis=1, tiled=True),
        lax.all_gather(value_low, "ctx", axis=1, tiled=True),
        lax.all_gather(segments.astype(jnp.bfloat16), "ctx", axis=1, tiled=True),
    )
    key_items = seq_items(key_all, local_kv)
    value_items = seq_items(value_all, local_kv)
    key_segments = jnp.repeat(segment_all.astype(jnp.int32), local_kv, axis=0)
    query_segments = jnp.repeat(jnp.repeat(segments, groups, axis=1), local_kv, axis=0)
    query_index = jnp.repeat(
        lax.axis_index("ctx") * span + jnp.arange(span, dtype=jnp.int32), groups
    )
    key_index = jnp.arange(key_all.shape[1], dtype=jnp.int32)
    query_blocks = to_blocks(query_rot, seq_count, local_kv, groups)

    def block_scores(block_query, block_keys, key_segment, query_segment):
        scores = (
            jnp.einsum("qd,kd->qk", block_query, block_keys, preferred_element_type=jnp.float32)
            * score_scale
        )
        allowed = (query_segment[:, None] == key_segment[None, :]) & (
            query_index[:, None] >= key_index[None, :]
        )
        return (scores, allowed)

    def forward_block(block_item):
        block_query, block_keys, block_values, key_segment, query_segment = block_item
        scores, allowed = block_scores(block_query, block_keys, key_segment, query_segment)
        scores = jnp.where(allowed, scores, NEGATIVE)
        row_max = jnp.max(scores, axis=1, keepdims=True)
        exp_scores = jnp.exp(scores - row_max)
        row_total = jnp.sum(exp_scores, axis=1, keepdims=True)
        attn_probs = (exp_scores / row_total).astype(jnp.bfloat16)
        mixed_block = jnp.dot(attn_probs, block_values, preferred_element_type=jnp.float32)
        return (mixed_block.astype(jnp.bfloat16), (row_max + jnp.log(row_total))[:, 0])

    mixed_blocks, row_lse = lax.map(
        forward_block, (query_blocks, key_items, value_items, key_segments, query_segments)
    )
    mixed_rows = from_blocks(mixed_blocks, seq_count, local_kv, groups)
    attended = lax.psum(jnp.dot(mixed_rows, attn_full[4], preferred_element_type=jnp.float32), "tp")
    residual = inputs + attended
    scale_mlp = inverse_rms(residual)
    normed_mlp = (residual * scale_mlp * mlp_full[0].astype(jnp.float32)).astype(jnp.bfloat16)
    gate_pre = jnp.dot(normed_mlp, mlp_full[1], preferred_element_type=jnp.float32)
    up_pre = jnp.dot(normed_mlp, mlp_full[2], preferred_element_type=jnp.float32)
    activated = jax.nn.silu(gate_pre)
    hidden = (activated * up_pre).astype(jnp.bfloat16)
    mlp_out = lax.psum(
        jnp.dot(hidden, mlp_full[3], preferred_element_type=jnp.float32).astype(jnp.bfloat16), "tp"
    ).astype(jnp.float32)
    layer_output = (residual + mlp_out).astype(jnp.bfloat16).reshape(seq_count, span, width)
    mlp_back = (
        lax.all_gather(mlp_gain, ("fsdp", "ctx"), axis=0, tiled=True),
        lax.all_gather(gate_proj, ("fsdp", "ctx"), axis=0, tiled=True),
        lax.all_gather(up_proj, ("fsdp", "ctx"), axis=0, tiled=True),
        lax.all_gather(down_proj, ("fsdp", "ctx"), axis=1, tiled=True),
    )
    upstream = out_grad.reshape(total_rows, width).astype(jnp.float32)
    upstream_low = upstream.astype(jnp.bfloat16)
    hidden_grad = contract(upstream_low, mlp_back[3], 1, 1)
    down_weight_grad = contract(hidden, upstream_low, 0, 0)
    sigmoid_gate = jax.nn.sigmoid(gate_pre)
    gate_grad = (
        hidden_grad * up_pre * sigmoid_gate * (1.0 + gate_pre * (1.0 - sigmoid_gate))
    ).astype(jnp.bfloat16)
    up_grad = (hidden_grad * activated).astype(jnp.bfloat16)
    normed_mlp_grad = lax.psum(
        contract(gate_grad, mlp_back[1], 1, 1) + contract(up_grad, mlp_back[2], 1, 1), "tp"
    )
    mlp_gain_term = jnp.sum(normed_mlp_grad * residual * scale_mlp, axis=0)
    residual_grad = norm_back(
        upstream, normed_mlp_grad * mlp_back[0].astype(jnp.float32), residual, scale_mlp
    )
    gate_weight_grad = contract(normed_mlp, gate_grad, 0, 0)
    up_weight_grad = contract(normed_mlp, up_grad, 0, 0)
    mlp_grads = (
        lax.psum_scatter(mlp_gain_term, ("fsdp", "ctx"), scatter_dimension=0, tiled=True),
        lax.psum_scatter(gate_weight_grad, ("fsdp", "ctx"), scatter_dimension=0, tiled=True),
        lax.psum_scatter(up_weight_grad, ("fsdp", "ctx"), scatter_dimension=0, tiled=True),
        lax.psum_scatter(down_weight_grad, ("fsdp", "ctx"), scatter_dimension=1, tiled=True),
    )
    attn_back = (
        lax.all_gather(attn_gain, ("fsdp", "ctx"), axis=0, tiled=True),
        lax.all_gather(query_proj, ("fsdp", "ctx"), axis=0, tiled=True),
        lax.all_gather(key_proj, ("fsdp", "ctx"), axis=0, tiled=True),
        lax.all_gather(value_proj, ("fsdp", "ctx"), axis=0, tiled=True),
        lax.all_gather(out_proj, ("fsdp", "ctx"), axis=1, tiled=True),
    )
    residual_low = residual_grad.astype(jnp.bfloat16)
    out_weight_grad = contract(mixed_rows, residual_low, 0, 0)
    mixed_grad = contract(residual_low, attn_back[4], 1, 1).astype(jnp.bfloat16)
    grad_blocks = to_blocks(mixed_grad, seq_count, local_kv, groups)

    def backward_block(block_item):
        block_query, block_keys, block_values, key_segment, query_segment, block_lse, block_grad = (
            block_item
        )
        scores, allowed = block_scores(block_query, block_keys, key_segment, query_segment)
        attn_probs = jnp.where(allowed, jnp.exp(scores - block_lse[:, None]), 0.0)
        prob_grad = jnp.einsum(
            "qd,kd->qk", block_grad, block_values, preferred_element_type=jnp.float32
        )
        row_delta = jnp.sum(prob_grad * attn_probs, axis=1, keepdims=True)
        score_grad = (attn_probs * (prob_grad - row_delta)).astype(jnp.bfloat16)
        value_grad = jnp.einsum(
            "qk,qd->kd",
            attn_probs.astype(jnp.bfloat16),
            block_grad,
            preferred_element_type=jnp.float32,
        )
        key_grad = (
            jnp.einsum("qk,qd->kd", score_grad, block_query, preferred_element_type=jnp.float32)
            * score_scale
        )
        query_grad = (
            jnp.dot(score_grad, block_keys, preferred_element_type=jnp.float32) * score_scale
        )
        return (query_grad, key_grad, value_grad)

    query_grads, key_grads, value_grads = lax.map(
        backward_block,
        (query_blocks, key_items, value_items, key_segments, query_segments, row_lse, grad_blocks),
    )
    key_back, value_back = (
        lax.psum_scatter(
            from_items(key_grads, seq_count, local_kv).astype(jnp.bfloat16),
            "ctx",
            scatter_dimension=1,
            tiled=True,
        ).astype(jnp.float32),
        lax.psum_scatter(
            from_items(value_grads, seq_count, local_kv).astype(jnp.bfloat16),
            "ctx",
            scatter_dimension=1,
            tiled=True,
        ).astype(jnp.float32),
    )
    query_grad_rows = (
        unrotate(
            from_blocks(query_grads, seq_count, local_kv, groups).reshape(total_rows, -1, DH),
            cos_table,
            sin_table,
        )
        .astype(jnp.bfloat16)
        .reshape(total_rows, -1)
    )
    key_grad_rows = (
        unrotate(key_back.reshape(total_rows, local_kv, DH), cos_table, sin_table)
        .astype(jnp.bfloat16)
        .reshape(total_rows, -1)
    )
    value_grad_rows = value_back.reshape(total_rows, -1).astype(jnp.bfloat16)
    query_weight_grad = contract(normed_attn, query_grad_rows, 0, 0)
    key_weight_grad = contract(normed_attn, key_grad_rows, 0, 0)
    value_weight_grad = contract(normed_attn, value_grad_rows, 0, 0)
    normed_partial = (
        contract(query_grad_rows, attn_back[1], 1, 1)
        + contract(key_grad_rows, attn_back[2], 1, 1)
        + contract(value_grad_rows, attn_back[3], 1, 1)
    )
    normed_attn_grad = lax.psum(normed_partial.astype(jnp.bfloat16), "tp").astype(jnp.float32)
    attn_gain_term = jnp.sum(normed_attn_grad * inputs * scale_attn, axis=0)
    input_grad = norm_back(
        residual_grad, normed_attn_grad * attn_back[0].astype(jnp.float32), inputs, scale_attn
    )
    attn_grads = (
        lax.psum_scatter(attn_gain_term, ("fsdp", "ctx"), scatter_dimension=0, tiled=True),
        lax.psum_scatter(query_weight_grad, ("fsdp", "ctx"), scatter_dimension=0, tiled=True),
        lax.psum_scatter(key_weight_grad, ("fsdp", "ctx"), scatter_dimension=0, tiled=True),
        lax.psum_scatter(value_weight_grad, ("fsdp", "ctx"), scatter_dimension=0, tiled=True),
        lax.psum_scatter(out_weight_grad, ("fsdp", "ctx"), scatter_dimension=1, tiled=True),
    )
    return (
        layer_output,
        input_grad.astype(jnp.bfloat16).reshape(seq_count, span, width),
        attn_grads[0],
        attn_grads[1],
        attn_grads[2],
        attn_grads[3],
        attn_grads[4],
        mlp_grads[0],
        mlp_grads[1],
        mlp_grads[2],
        mlp_grads[3],
    )


def solution(mesh):
    return jax.shard_map(
        on_device,
        mesh=mesh,
        in_specs=(
            P("fsdp", "ctx", None),
            P("fsdp", "ctx"),
            P("fsdp", "ctx"),
            P(("fsdp", "ctx")),
            P(("fsdp", "ctx"), "tp"),
            P(("fsdp", "ctx"), "tp"),
            P(("fsdp", "ctx"), "tp"),
            P("tp", ("fsdp", "ctx")),
            P(("fsdp", "ctx")),
            P(("fsdp", "ctx"), "tp"),
            P(("fsdp", "ctx"), "tp"),
            P("tp", ("fsdp", "ctx")),
            P("fsdp", "ctx", None),
        ),
        out_specs=(
            P("fsdp", "ctx", None),
            P("fsdp", "ctx", None),
            P(("fsdp", "ctx")),
            P(("fsdp", "ctx"), "tp"),
            P(("fsdp", "ctx"), "tp"),
            P(("fsdp", "ctx"), "tp"),
            P("tp", ("fsdp", "ctx")),
            P(("fsdp", "ctx")),
            P(("fsdp", "ctx"), "tp"),
            P(("fsdp", "ctx"), "tp"),
            P("tp", ("fsdp", "ctx")),
        ),
        check_vma=False,
    )
```

profile of v0, /device:TPU:0, one launch (start us, length us, event | category | flops | bytes accessed | tf_op | source)
XLA Modules:
  0.0 1363.1 jit_solution(13727046639164746978)
XLA Ops:
  12.3 12.6 all_gather.45
  28.6 31.5 %all-reduce.5 = (bf16[1536]{0:T(1024)(128)(2,1)S(1)}, bf16[1536]{0:T(1024)(128)(2,1)}) all-reduce(bf16[1536]{0:T(1024)(128)(2,1)S(1)} %dynamic-update-slice, bf16[1536]{0:T(1024)(128)(2,1)S(1)} %dynamic-update-slice.1), channel_id=1, replica_groups=mesh['fsdp'=4,'ctx'=4,'tp'=2] {'fsdp','ctx'}, use_global_device_ids=true, to_apply=%add | all-reduce | flops 3072 | bytes 12288
  62.4 1.6 copy.51
  64.6 19.5 %all_gather.49 = bf16[1,1024,384]{1,2,0:T(8,128)(2,1)S(1)} all-gather(bf16[1,256,384]{1,2,0:T(8,128)(2,1)S(1)} %bitcast.263), channel_id=1, replica_groups=mesh['fsdp'=4,'ctx'=4,'tp'=2] {'ctx'}, dimensions={1}, use_global_device_ids=true | all-gather | bytes 983040 | tf_op jit(solution)/shard_map/all_gather | solution.py:152
  84.9 7.7 all-gather.13.cloned.1.call-done
  92.6 1.9 convolution_convert_fusion.3
  94.4 22.7 %all-gather = bf16[1024,384]{1,0:T(8,128)(2,1)S(1)} all-gather(bf16[256,384]{1,0:T(8,128)(2,1)S(1)} %convolution_convert_fusion.3), channel_id=2, replica_groups=mesh['fsdp'=4,'ctx'=4,'tp'=2] {'ctx'}, dimensions={0}, use_global_device_ids=true | all-gather | bytes 983040 | tf_op jit(solution)/shard_map/all_gather | solution.py:153
  117.6 20.4 %all-gather.9.cloned.1.call-done = bf16[1536,768]{1,0:T(8,128)(2,1)} async-done(((bf16[96,768]{1,0:T(8,128)(2,1)}), bf16[1536,768]{1,0:T(8,128)(2,1)}) %all-gather.9.cloned.1.call-update) | async-done | bytes 2359312 | tf_op jit(solution)/shard_map/all_gather | solution.py:115
  138.1 4.3 copy.49
  142.3 2.6 fusion.77
  148.3 22.3 %while.28 = (s32[]{:T(128)}, bf16[4,512,96]{1,2,0:T(8,128)(2,1)}, f32[4,512]{1,0:T(4,128)}, s32[4,512]{1,0:T(4,128)}, s32[4,1024]{1,0:T(4,128)}, /*index=5*/bf16...) while((s32[]{:T(128)}, bf16[4,512,96]{1,2,0:T(8,128)(2,1)}, ...), condition=%wide.region_4.5_spmd.clone, body=%wide.region_1.4_spmd.clone.sunk | while | flops 207142400 | bytes 7095425 | solution.py:187
  170.6 2.3 copy.53
  174.2 7.3 all-gather.15.cloned.1.call-done
  181.4 3.7 fusion.102
  187.4 48.1 %all-reduce.11.cloned.1.call-done = f32[256,1536]{1,0:T(8,128)} async-done(((f32[256,1536]{1,0:T(8,128)}), f32[256,1536]{1,0:T(8,128)}) %all-reduce.11.cloned.1.call-update) | async-done | bytes 1572880 | tf_op jit(solution)/shard_map/psum | solution.py:191
  235.5 1.7 multiply_reduce_fusion.3
  237.4 62.4 %all-gather.17.cloned.1.call-done = bf16[1536,2048]{1,0:T(8,128)(2,1)} async-done(((bf16[96,2048]{1,0:T(8,128)(2,1)}), bf16[1536,2048]{1,0:T(8,128)(2,1)}) %all-gather.17.cloned.1.call-update) | async-done | bytes 6291472 | tf_op jit(solution)/shard_map/all_gather | solution.py:122
  299.9 6.0 fusion.103
  305.8 57.1 %all-gather.19.cloned.1.call-done = bf16[1536,2048]{1,0:T(8,128)(2,1)} async-done(((bf16[96,2048]{1,0:T(8,128)(2,1)}), bf16[1536,2048]{1,0:T(8,128)(2,1)}) %all-gather.19.cloned.1.call-update) | async-done | bytes 6291472 | tf_op jit(solution)/shard_map/all_gather | solution.py:123
  362.9 5.9 fusion.104
  368.8 57.2 %all-gather.21.cloned.1.call-done = bf16[2048,1536]{0,1:T(8,128)(2,1)} async-done(((bf16[2048,96]{0,1:T(8,128)(2,1)}), bf16[2048,1536]{0,1:T(8,128)(2,1)}) %all-gather.21.cloned.1.call-update) | async-done | bytes 6291472 | tf_op jit(solution)/shard_map/all_gather | solution.py:124
  426.0 7.6 multiply_convert_fusion.1
  433.6 5.4 fusion.105
  439.1 3.0 convolution_add_fusion.2
  442.4 49.9 %all-reduce.13.cloned.1.call-done = f32[256,1536]{1,0:T(8,128)} async-done(((f32[256,1536]{1,0:T(8,128)}), f32[256,1536]{1,0:T(8,128)}) %all-reduce.13.cloned.1.call-update) | async-done | bytes 1572880 | tf_op jit(solution)/shard_map/psum | solution.py:218
  492.3 2.5 multiply_reduce_fusion.1
  498.8 2.0 copy.56
  500.8 42.8 %while.29 = (s32[]{:T(128)}, f32[4,512,96]{1,2,0:T(8,128)}, bf16[4,1024,96]{1,2,0:T(8,128)(2,1)}, bf16[4,1024,96]{1,2,0:T(8,128)(2,1)}, s32[4,512]{1,0:T(4,128)}...) while((s32[]{:T(128)}, f32[4,512,96]{1,2,0:T(8,128)}, ...), condition=%wide.region_12.13_spmd.clone, body=%wide.region_10.12_spmd.clone.sunk | while | flops 509754880 | bytes 32221468 | solution.py:271
  503.2 1.9 exponential_select_fusion.2
  505.1 1.5 multiply_reduce_fusion.5
  506.8 2.2 fusion.168
  513.9 1.9 exponential_select_fusion.2
  517.5 2.2 fusion.168
  524.6 1.9 exponential_select_fusion.2
  526.5 1.5 multiply_reduce_fusion.5
  528.2 2.2 fusion.168
  535.3 1.9 exponential_select_fusion.2
  537.2 1.5 multiply_reduce_fusion.5
  538.9 2.2 fusion.168
  544.4 5.8 convolution_convert_fusion.1
  550.2 2.5 copy.57
  552.7 2.2 copy.58
  556.2 3.7 fusion.106
  559.8 7.1 reduce-scatter.10.cloned.1.call-done
  569.6 3.1 convolution_add_fusion.1
  572.6 20.0 %reduce-scatter.12.cloned.1.call-done = bf16[1,256,384]{1,2,0:T(8,128)(2,1)} async-done(((bf16[1,1024,384]{1,2,0:T(8,128)(2,1)}), bf16[1,256,384]{1,2,0:T(8,128)(2,1)}) %reduce-scatter.12.cloned.1.call-update) | async-done | bytes 196624 | tf_op jit(solution)/shard_map/reduce_scatter | solution.py:282
  592.6 3.3 fusion.47
  596.6 3.0 fusion.83
  599.7 3.1 fusion.81
  602.8 3.1 fusion.79
  606.9 4.5 fusion.87
  611.7 7.6 fusion.107
  619.4 7.6 fusion.108
  628.2 7.8 fusion.71
  636.6 10.4 all-reduce.15.cloned.1.call-done
  647.0 1.7 fusion.65
  648.7 61.8 %all-reduce.4 = (f32[1536]{0:T(1024)S(1)}, f32[1536]{0:T(1024)S(1)}) all-reduce(f32[1536]{0:T(1024)S(1)} %get-tuple-element.190, f32[1536]{0:T(1024)S(1)} %copy-done.27), channel_id=5, replica_groups=mesh['fsdp'=4,'ctx'=4,'tp'=2] {'fsdp','ctx'}, use_global_device_ids=true, to_apply=%region_18.19.clone | all-reduce | flops 3072 | bytes 24576
  711.6 3.3 fusion.68
  715.1 66.1 %reduce-scatter.18.cloned.1.call-done = f32[96,384]{1,0:T(8,128)} async-done(((f32[1536,384]{1,0:T(8,128)}), f32[96,384]{1,0:T(8,128)}) %reduce-scatter.18.cloned.1.call-update) | async-done | bytes 147472 | tf_op jit(solution)/shard_map/reduce_scatter | solution.py:321
  781.3 79.4 %reduce-scatter.14.cloned.1.call-done = f32[96,768]{1,0:T(8,128)} async-done(((f32[1536,768]{1,0:T(8,128)}), f32[96,768]{1,0:T(8,128)}) %reduce-scatter.14.cloned.1.call-update) | async-done | bytes 294928 | tf_op jit(solution)/shard_map/reduce_scatter | solution.py:319
  860.7 78.9 %reduce-scatter.20.cloned.1.call-done = f32[768,96]{0,1:T(8,128)} async-done(((f32[768,1536]{0,1:T(8,128)}), f32[768,96]{0,1:T(8,128)}) %reduce-scatter.20.cloned.1.call-update) | async-done | bytes 294928 | tf_op jit(solution)/shard_map/reduce_scatter | solution.py:322
  939.6 138.8 %reduce-scatter.22.cloned.1.call-done = f32[96,2048]{1,0:T(8,128)} async-done(((f32[1536,2048]{1,0:T(8,128)}), f32[96,2048]{1,0:T(8,128)}) %reduce-scatter.22.cloned.1.call-update) | async-done | bytes 786448 | tf_op jit(solution)/shard_map/reduce_scatter | solution.py:229
  1078.4 139.0 %reduce-scatter.24.cloned.1.call-done = f32[96,2048]{1,0:T(8,128)} async-done(((f32[1536,2048]{1,0:T(8,128)}), f32[96,2048]{1,0:T(8,128)}) %reduce-scatter.24.cloned.1.call-update) | async-done | bytes 786448 | tf_op jit(solution)/shard_map/reduce_scatter | solution.py:230
  1217.4 139.1 %reduce-scatter.26.cloned.1.call-done = f32[2048,96]{0,1:T(8,128)} async-done(((f32[2048,1536]{0,1:T(8,128)}), f32[2048,96]{0,1:T(8,128)}) %reduce-scatter.26.cloned.1.call-update) | async-done | bytes 786448 | tf_op jit(solution)/shard_map/reduce_scatter | solution.py:231
  (255 shorter events, 77.2 us)
Async XLA Ops:
  7.2 54.9 %copy-start.31 = (s32[1,256]{1,0:T(1,128)S(1)}, s32[1,256]{1,0:T(1,128)}, u32[]{:S(2)}) copy-start(s32[1,256]{1,0:T(1,128)} %param.19) | copy-start | bytes 3076
  7.2 55.2 %all-gather.11.cloned.1.call-start = ((), (), s32[]{:S(2)}) async-start(), calls=%async_computation.10 | async-start | bytes 1253376 | tf_op jit(solution)/shard_map/all_gather | solution.py:116
  7.9 84.6 %all-gather.13.cloned.1.call-start = ((), (), s32[]{:S(2)}) async-start(), calls=%async_computation.11 | async-start | bytes 1253376 | tf_op jit(solution)/shard_map/all_gather | solution.py:117
  8.7 129.4 %all-gather.9.cloned.1.call-start = ((), (), s32[]{:S(2)}) async-start(), calls=%async_computation.9 | async-start | bytes 2506752 | tf_op jit(solution)/shard_map/all_gather | solution.py:115
  9.4 172.0 %all-gather.15.cloned.1.call-start = ((), (), s32[]{:S(2)}) async-start(), calls=%async_computation.12 | async-start | bytes 2506752 | tf_op jit(solution)/shard_map/all_gather | solution.py:118
  10.0 225.6 %all-reduce.11.cloned.1.call-start = ((), (), s32[]{:S(2)}) async-start(), calls=%async_computation.13 | async-start | bytes 3145728 | tf_op jit(solution)/shard_map/psum | solution.py:191
  60.1 3.9 copy-start
  62.1 80.3 %copy-start.25 = (f32[256]{0:T(256)}, f32[256]{0:T(256)S(1)}, u32[]{:S(2)}) copy-start(f32[256]{0:T(256)S(1)} %get-tuple-element.268) | copy-start | bytes 3076
  62.3 82.6 %copy-start.15 = (f32[256,48]{0,1:T(8,128)}, f32[256,48]{0,1:T(8,128)S(1)}, u32[]{:S(2)}) copy-start(f32[256,48]{0,1:T(8,128)S(1)} %get-tuple-element.265) | copy-start | bytes 147460
  62.3 82.6 %copy-start.17 = (f32[256,48]{0,1:T(8,128)}, f32[256,48]{0,1:T(8,128)S(1)}, u32[]{:S(2)}) copy-start(f32[256,48]{0,1:T(8,128)S(1)} %get-tuple-element.266) | copy-start | bytes 147460
  144.9 2.2 copy-start.28
  170.6 2.3 copy-start.13
  170.6 14.4 %copy-start.6 = (bf16[4,1024,96]{2,1,0:T(8,128)(2,1)}, bf16[4,1024,96]{2,1,0:T(8,128)(2,1)S(1)}, u32[]{:S(2)}) copy-start(bf16[4,1024,96]{2,1,0:T(8,128)(2,1)S(1)} %get-tuple-element.524) | copy-start | bytes 2359300
  170.6 14.4 %copy-start.7 = (bf16[4,1024,96]{2,1,0:T(8,128)(2,1)}, bf16[4,1024,96]{2,1,0:T(8,128)(2,1)S(1)}, u32[]{:S(2)}) copy-start(bf16[4,1024,96]{2,1,0:T(8,128)(2,1)S(1)} %get-tuple-element.525) | copy-start | bytes 2359300
  174.1 10.9 copy-start.8
  185.1 2.3 copy-start.30
  185.1 114.7 %all-gather.17.cloned.1.call-start = ((), (), s32[]{:S(2)}) async-start(), calls=%async_computation.14 | async-start | bytes 6684672 | tf_op jit(solution)/shard_map/all_gather | solution.py:122
  185.7 177.2 %all-gather.19.cloned.1.call-start = ((), (), s32[]{:S(2)}) async-start(), calls=%async_computation.15 | async-start | bytes 6684672 | tf_op jit(solution)/shard_map/all_gather | solution.py:123
  186.4 239.5 %all-gather.21.cloned.1.call-start = ((), (), s32[]{:S(2)}) async-start(), calls=%async_computation.16 | async-start | bytes 6684672 | tf_op jit(solution)/shard_map/all_gather | solution.py:124
  187.2 305.1 %all-reduce.13.cloned.1.call-start = ((), (), s32[]{:S(2)}) async-start(), calls=%async_computation.17 | async-start | bytes 3145728 | tf_op jit(solution)/shard_map/psum | solution.py:218
  433.6 5.4 copy-start.20
  433.6 5.4 copy-start.19
  433.6 5.4 copy-start.32
  442.1 124.8 %reduce-scatter.10.cloned.1.call-start = ((), (), s32[]{:S(2)}) async-start(), calls=%async_computation.18 | async-start | bytes 983040 | tf_op jit(solution)/shard_map/reduce_scatter | solution.py:276
  492.3 2.6 copy-start.5
  492.3 2.6 copy-start.10
  494.9 2.2 copy-start.2
  495.4 1.2 copy-start.1
  503.2 1.9 copy-start.3
  506.6 2.4 copy-start.21
  506.8 3.5 copy-start.23
  510.3 0.9 copy-start.22
  510.6 0.9 copy-start.24
  513.9 1.9 copy-start.3
  517.3 2.4 copy-start.21
  517.5 3.5 copy-start.23
  521.0 0.9 copy-start.22
  521.3 0.9 copy-start.24
  524.6 1.9 copy-start.3
  527.9 2.4 copy-start.21
  528.2 3.5 copy-start.23
  531.6 0.9 copy-start.22
  532.0 0.9 copy-start.24
  535.3 1.9 copy-start.3
  538.6 2.4 copy-start.21
  538.9 3.5 copy-start.23
  542.3 0.9 copy-start.22
  543.6 49.0 %reduce-scatter.12.cloned.1.call-start = ((), (), s32[]{:S(2)}) async-start(), calls=%async_computation.19 | async-start | bytes 983040 | tf_op jit(solution)/shard_map/reduce_scatter | solution.py:282
  544.4 102.6 %all-reduce.15.cloned.1.call-start = ((), (), s32[]{:S(2)}) async-start(), calls=%async_computation.27 | async-start | bytes 3145728 | tf_op jit(solution)/shard_map/psum | solution.py:199
  550.2 4.7 copy-start.16
  550.2 4.7 copy-start.18
  566.9 2.7 copy-start.4
  596.0 119.2 %reduce-scatter.16.cloned.1.call-start = ((), (), s32[]{:S(2)}) async-start(), calls=%async_computation.21 | async-start | bytes 2506752 | tf_op jit(solution)/shard_map/reduce_scatter | solution.py:320
  599.6 181.6 %reduce-scatter.18.cloned.1.call-start = ((), (), s32[]{:S(2)}) async-start(), calls=%async_computation.22 | async-start | bytes 2506752 | tf_op jit(solution)/shard_map/reduce_scatter | solution.py:321
  602.8 257.9 %reduce-scatter.14.cloned.1.call-start = ((), (), s32[]{:S(2)}) async-start(), calls=%async_computation.20 | async-start | bytes 5013504 | tf_op jit(solution)/shard_map/reduce_scatter | solution.py:319
  605.9 1.0 copy-start.9
  605.9 333.7 %reduce-scatter.20.cloned.1.call-start = ((), (), s32[]{:S(2)}) async-start(), calls=%async_computation.23 | async-start | bytes 5013504 | tf_op jit(solution)/shard_map/reduce_scatter | solution.py:322
  611.4 467.1 %reduce-scatter.22.cloned.1.call-start = ((), (), s32[]{:S(2)}) async-start(), calls=%async_computation.24 | async-start | bytes 13369344 | tf_op jit(solution)/shard_map/reduce_scatter | solution.py:229
  619.3 598.1 %reduce-scatter.24.cloned.1.call-start = ((), (), s32[]{:S(2)}) async-start(), calls=%async_computation.25 | async-start | bytes 13369344 | tf_op jit(solution)/shard_map/reduce_scatter | solution.py:230
  626.9 1.2 copy-start.11
  627.0 729.6 %reduce-scatter.26.cloned.1.call-start = ((), (), s32[]{:S(2)}) async-start(), calls=%async_computation.26 | async-start | bytes 13369344 | tf_op jit(solution)/shard_map/reduce_scatter | solution.py:231
  635.9 12.7 copy-start.27
  635.9 75.7 %copy-start.29 = (f32[256]{0:T(256)S(1)}, f32[256]{0:T(256)}, u32[]{:S(2)}) copy-start(f32[256]{0:T(256)} %get-tuple-element.267) | copy-start | bytes 3076
  647.0 64.6 %copy-start.12 = (bf16[256,1536]{1,0:T(8,128)(2,1)S(1)}, bf16[256,1536]{1,0:T(8,128)(2,1)}, u32[]{:S(2)}) copy-start(bf16[256,1536]{1,0:T(8,128)(2,1)} %get-tuple-element.239) | copy-start | bytes 2359300
  (3 other events, 2.2 us)
Sparse Core Ops, SparseCore 0:
  10.3 41.3 all-gather.10
  54.0 38.4 all-gather.12
  94.9 43.1 all-gather.8
  140.2 41.1 all-gather.14
  185.2 50.2 all-reduce.10
  238.0 61.8 all-gather.16
  302.4 60.4 all-gather.18
  365.5 60.4 all-gather.20
  442.2 50.0 all-reduce.12
  543.7 23.1 reduce-scatter.9
  569.8 22.7 reduce-scatter.11
  596.1 50.8 all-reduce.14
  651.8 63.2 reduce-scatter.15
  719.3 61.9 reduce-scatter.17
  786.0 74.5 reduce-scatter.13
  865.0 74.5 reduce-scatter.19
  944.6 133.7 reduce-scatter.21
  1083.4 133.9 reduce-scatter.23
  1222.6 133.8 reduce-scatter.25
where the time goes:
time: 1370 us; the launch traced here: 1360 us
  waiting for transfers between devices  994 us (73%)
  blocking collectives  148 us (11%)
  matrix products  127 us (9%)
  local copies, waits for them, and re-layouts  56.2 us (4%)
  other arithmetic  20.3 us (1%)
  between operations  15.7 us (1%)
    reduce_scatter x1, waiting for transfers between devices, on_device(): lax.psum_scatter(down_weight_grad, ('fsdp', 'ctx'), scatter_dimension=1,...  139 us
    reduce_scatter x1, waiting for transfers between devices, on_device(): lax.psum_scatter(up_weight_grad, ('fsdp', 'ctx'), scatter_dimension=0, ti...  139 us
    reduce_scatter x1, waiting for transfers between devices, on_device(): lax.psum_scatter(gate_weight_grad, ('fsdp', 'ctx'), scatter_dimension=0,...  139 us
    unnamed x2, blocking collectives  93.2 us
    reduce_scatter x1, waiting for transfers between devices, on_device(): lax.psum_scatter(query_weight_grad, ('fsdp', 'ctx'), scatter_dimension=0,...  79.4 us
    reduce_scatter x1, waiting for transfers between devices, on_device(): lax.psum_scatter(out_weight_grad, ('fsdp', 'ctx'), scatter_dimension=1, t...  78.9 us
    reduce_scatter x1, waiting for transfers between devices, on_device(): lax.psum_scatter(value_weight_grad, ('fsdp', 'ctx'), scatter_dimension=0,...  66.1 us
    dot_general x14, matrix products, contract(): lax.dot_general(left, right, (((left_dim,), (right_dim,)), ((), ())), pre...  63.5 us
  transfers between devices with their start and end apart: 19, of which 18 were waited for; matrix products, arithmetic and copies ran while one was open for 9% of the time, Pallas kernels for 0%

commit v1 on v0

--- a/solution.py
+++ b/solution.py
@@ -1,3 +1,4 @@
+import functools
 import jax
 import jax.numpy as jnp
 from jax import lax
@@ -9,6 +10,39 @@
 EPS = 1e-05
 THETA = 100000.0
 NEGATIVE = -1e30
+
+
+def advance_the_figure(local_x, dim_i):
+    local_x = jnp.moveaxis(local_x, 0, dim_i)
+    arr_out = local_x.shape
+    current_value = local_x.reshape(
+        *arr_out[:dim_i], arr_out[dim_i] * arr_out[dim_i + 1], *arr_out[dim_i + 2 :]
+    )
+    return current_value
+
+
+def axis_part_start(unit, mesh_name, pos_dim):
+    n_lanes = lax.axis_size(mesh_name)
+    steps_seen = [(dev_j, (dev_j + 1) % n_lanes) for dev_j in range(n_lanes)]
+    pieces_in = [(dd, dev_i) for dev_i, dd in steps_seen]
+    d_next, high = ([], [])
+    for to_i in [*range(n_lanes - 1)]:
+        if to_i % 2 == 0:
+            left_arr = lax.ppermute(d_next[-1] if d_next else unit, mesh_name, steps_seen)
+            d_next.append(left_arr)
+        else:
+            all_rows = lax.ppermute(high[-1] if high else unit, mesh_name, pieces_in)
+            high.append(all_rows)
+    latest = jnp.stack([*d_next[::-1], unit, *high], axis=0)
+    p_next = lax.axis_index(mesh_name)
+    then = len(d_next)
+    val2 = p_next - then
+    latest = latest[(jnp.arange(n_lanes) - val2) % n_lanes]
+    low = advance_the_figure(latest, pos_dim)
+    return low
+
+
+turn_routes_all = functools.partial(axis_part_start, mesh_name=("fsdp", "ctx"), pos_dim=0)
 
 
 def rotary_tables(positions):
@@ -120,7 +154,7 @@
     mlp_full = (
         lax.all_gather(mlp_gain, ("fsdp", "ctx"), axis=0, tiled=True),
         lax.all_gather(gate_proj, ("fsdp", "ctx"), axis=0, tiled=True),
-        lax.all_gather(up_proj, ("fsdp", "ctx"), axis=0, tiled=True),
+        turn_routes_all(up_proj),
         lax.all_gather(down_proj, ("fsdp", "ctx"), axis=1, tiled=True),
     )
     seq_count, span, width = layer_input.shape

time: 1370 us -> 1410 us (1.029)
  starting transfers between devices: 1.42 us -> 25.7 us
    ppermute x0 -> x15, waiting for transfers between devices: none -> 149 us  [the longest x7 96.5 us: axis_part_start(): all_rows = lax.ppermute(high[-1] if high else unit, mesh_name, pieces_in)]
    all_gather x1, waiting for transfers between devices: 62.4 us -> 0.02 us  [on_device(): lax.all_gather(gate_proj, ('fsdp', 'ctx'), axis=0, tiled=True)]
    psum x1, waiting for transfers between devices: 48.1 us -> 0.01 us  [on_device(): lax.psum(jnp.dot(mixed_rows, attn_full[4], preferred_element_type=jnp.flo...]
    all_gather x1, waiting for transfers between devices: 57.2 us -> 16.8 us  [on_device(): lax.all_gather(down_proj, ('fsdp', 'ctx'), axis=1, tiled=True)]
    ppermute x0 -> x15, starting transfers between devices: none -> 24.5 us  [the longest x8 14 us: axis_part_start(): lax.ppermute(d_next[-1] if d_next else unit, mesh_name, steps_seen)]
    unnamed x63 -> x96, local copies, waits for them, and re-layouts: 9.38 us -> 26.9 us
  transfers between devices with their start and end apart: 19 -> 34, of which waited for: 18 -> 29; matrix products, arithmetic and copies ran while one was open for 9% -> 11% of each run, Pallas kernels for 0% -> 0%
where the time goes in v1:
time: 1410 us; the launch traced here: 1400 us
  waiting for transfers between devices  988 us (70%)
  blocking collectives  148 us (10%)
  matrix products  134 us (10%)
  local copies, waits for them, and re-layouts  70.3 us (5%)
  starting transfers between devices  25.7 us (2%)
  other arithmetic  21.6 us (2%)
  between operations  16.1 us (1%)
    reduce_scatter x1, waiting for transfers between devices, on_device(): lax.psum_scatter(down_weight_grad, ('fsdp', 'ctx'), scatter_dimension=1,...  139 us
    reduce_scatter x1, waiting for transfers between devices, on_device(): lax.psum_scatter(gate_weight_grad, ('fsdp', 'ctx'), scatter_dimension=0,...  139 us
    reduce_scatter x1, waiting for transfers between devices, on_device(): lax.psum_scatter(up_weight_grad, ('fsdp', 'ctx'), scatter_dimension=0, ti...  139 us
    unnamed x2, blocking collectives  98.8 us
    ppermute x7, waiting for transfers between devices, axis_part_start(): all_rows = lax.ppermute(high[-1] if high else unit, mesh_name, pieces_in)  96.5 us
    reduce_scatter x1, waiting for transfers between devices, on_device(): lax.psum_scatter(out_weight_grad, ('fsdp', 'ctx'), scatter_dimension=1, t...  79.4 us
    reduce_scatter x1, waiting for transfers between devices, on_device(): lax.psum_scatter(query_weight_grad, ('fsdp', 'ctx'), scatter_dimension=0,...  78.9 us
    reduce_scatter x1, waiting for transfers between devices, on_device(): lax.psum_scatter(value_weight_grad, ('fsdp', 'ctx'), scatter_dimension=0,...  66.1 us
  transfers between devices with their start and end apart: 34, of which 29 were waited for; matrix products, arithmetic and copies ran while one was open for 11% of the time, Pallas kernels for 0%

profile of v1, /device:TPU:0, one launch (start us, length us, event | category | flops | bytes accessed | tf_op | source)
XLA Modules:
  0.0 1403.6 jit_solution(12557821370029504824)
XLA Ops:
  13.8 37.0 %all-reduce.5 = (bf16[1536]{0:T(1024)(128)(2,1)S(1)}, bf16[1536]{0:T(1024)(128)(2,1)}) all-reduce(bf16[1536]{0:T(1024)(128)(2,1)S(1)} %dynamic-update-slice, bf16[1536]{0:T(1024)(128)(2,1)S(1)} %dynamic-update-slice.1), channel_id=1, replica_groups=mesh['fsdp'=4,'ctx'=4,'tp'=2] {'fsdp','ctx'}, use_global_device_ids=true, to_apply=%add | all-reduce | flops 3072 | bytes 12288
  55.1 7.6 all_gather.44
  65.3 18.8 %all_gather.48 = bf16[1,1024,384]{1,2,0:T(8,128)(2,1)S(1)} all-gather(bf16[1,256,384]{1,2,0:T(8,128)(2,1)S(1)} %bitcast.296), channel_id=1, replica_groups=mesh['fsdp'=4,'ctx'=4,'tp'=2] {'ctx'}, dimensions={1}, use_global_device_ids=true | all-gather | bytes 983040 | tf_op jit(solution)/shard_map/all_gather | solution.py:186
  85.5 7.2 all-gather.13.cloned.1.call-done
  94.6 22.6 %all-gather = bf16[1024,384]{1,0:T(8,128)(2,1)S(1)} all-gather(bf16[256,384]{1,0:T(8,128)(2,1)S(1)} %convolution_convert_fusion.3), channel_id=2, replica_groups=mesh['fsdp'=4,'ctx'=4,'tp'=2] {'ctx'}, dimensions={0}, use_global_device_ids=true | all-gather | bytes 983040 | tf_op jit(solution)/shard_map/all_gather | solution.py:187
  118.7 19.6 %all-gather.9.cloned.1.call-done = bf16[1536,768]{1,0:T(8,128)(2,1)} async-done(((bf16[96,768]{1,0:T(8,128)(2,1)}), bf16[1536,768]{1,0:T(8,128)(2,1)}) %all-gather.9.cloned.1.call-update) | async-done | bytes 2359312 | tf_op jit(solution)/shard_map/all_gather | solution.py:149
  138.3 2.8 copy.49
  142.6 24.1 %while.28 = (s32[]{:T(128)}, bf16[4,512,96]{1,2,0:T(8,128)(2,1)}, f32[4,512]{1,0:T(4,128)}, s32[4,512]{1,0:T(4,128)S(1)}, s32[4,1024]{1,0:T(4,128)S(1)}, /*index...) while((s32[]{:T(128)}, bf16[4,512,96]{1,2,0:T(8,128)(2,1)}, ...), condition=%wide.region_4.5_spmd.clone, body=%wide.region_1.4_spmd.clone.sunk | while | flops 207142400 | bytes 7095417 | solution.py:221
  146.4 2.2 fusion.160
  168.5 13.0 all-gather.15.cloned.1.call-done
  181.5 3.6 fusion.104
  187.6 12.6 collective-permute-done
  200.3 4.4 collective-permute-start.8
  204.7 9.7 collective-permute-done.1
  214.4 5.0 collective-permute-done.8
  219.4 3.5 collective-permute-start.9
  222.9 8.4 collective-permute-done.2
  231.3 6.4 collective-permute-done.9
  239.8 8.3 collective-permute-done.3
  248.2 26.3 %collective-permute-done.10 = bf16[96,2048]{1,0:T(8,128)(2,1)S(1)} collective-permute-done((bf16[96,2048]{1,0:T(8,128)(2,1)S(1)}, bf16[96,2048]{1,0:T(8,128)(2,1)S(1)}, u32[]{:S(2)}, u32[]{:S(2)}) %collective-permute-start.10) | collective-permute-done | bytes 393248 | tf_op jit(solution)/shard_map/ppermute | solution.py:34
  274.5 3.2 collective-permute-done.4
  277.7 21.4 %collective-permute-done.11 = bf16[96,2048]{1,0:T(8,128)(2,1)S(1)} collective-permute-done((bf16[96,2048]{1,0:T(8,128)(2,1)S(1)}, bf16[96,2048]{1,0:T(8,128)(2,1)S(1)}, u32[]{:S(2)}, u32[]{:S(2)}) %collective-permute-start.11) | collective-permute-done | bytes 393248 | tf_op jit(solution)/shard_map/ppermute | solution.py:34
  299.1 5.1 collective-permute-done.5
  304.2 10.9 collective-permute-start.6
  315.2 21.5 %collective-permute-done.12 = bf16[96,2048]{1,0:T(8,128)(2,1)} collective-permute-done((bf16[96,2048]{1,0:T(8,128)(2,1)S(1)}, bf16[96,2048]{1,0:T(8,128)(2,1)}, u32[]{:S(2)}, u32[]{:S(2)}) %collective-permute-start.12) | collective-permute-done | bytes 393248 | tf_op jit(solution)/shard_map/ppermute | solution.py:34
  340.1 15.8 %collective-permute-done.13 = bf16[96,2048]{1,0:T(8,128)(2,1)} collective-permute-done((bf16[96,2048]{1,0:T(8,128)(2,1)}, bf16[96,2048]{1,0:T(8,128)(2,1)}, u32[]{:S(2)}, u32[]{:S(2)}) %collective-permute-start.13) | collective-permute-done | bytes 393248 | tf_op jit(solution)/shard_map/ppermute | solution.py:34
  356.3 4.9 collective-permute-done.7
  378.7 6.5 gather_fusion
  387.2 5.9 fusion.105
  393.1 16.8 %all-gather.19.cloned.1.call-done = bf16[2048,1536]{0,1:T(8,128)(2,1)} async-done(((bf16[2048,96]{0,1:T(8,128)(2,1)}), bf16[2048,1536]{0,1:T(8,128)(2,1)}) %all-gather.19.cloned.1.call-update) | async-done | bytes 6291472 | tf_op jit(solution)/shard_map/all_gather | solution.py:158
  409.9 5.0 fusion.73
  414.9 6.8 multiply_convert_fusion.1
  422.7 3.0 fusion.106
  425.7 47.3 %all-gather.21.cloned.1.call-done = bf16[1536,2048]{1,0:T(8,128)(2,1)} async-done(((bf16[96,2048]{1,0:T(8,128)(2,1)}), bf16[1536,2048]{1,0:T(8,128)(2,1)}) %all-gather.21.cloned.1.call-update) | async-done | bytes 6291472 | tf_op jit(solution)/shard_map/all_gather | solution.py:240
  473.0 6.5 convolution_add_fusion.2
  479.7 50.0 %all-reduce.13.cloned.1.call-done = f32[256,1536]{1,0:T(8,128)} async-done(((f32[256,1536]{1,0:T(8,128)}), f32[256,1536]{1,0:T(8,128)}) %all-reduce.13.cloned.1.call-update) | async-done | bytes 1572880 | tf_op jit(solution)/shard_map/psum | solution.py:252
  529.7 2.6 multiply_reduce_fusion.1
  538.2 45.9 %while.29 = (s32[]{:T(128)}, f32[4,512,96]{1,2,0:T(8,128)}, bf16[4,1024,96]{1,2,0:T(8,128)(2,1)}, bf16[4,1024,96]{1,2,0:T(8,128)(2,1)}, s32[4,512]{1,0:T(4,128)}...) while((s32[]{:T(128)}, f32[4,512,96]{1,2,0:T(8,128)}, ...), condition=%wide.region_12.13_spmd.clone, body=%wide.region_10.12_spmd.clone.sunk | while | flops 509754880 | bytes 25929948 | solution.py:305
  546.4 2.3 fusion.169
  557.9 2.3 fusion.169
  569.3 2.3 fusion.169
  580.8 2.3 fusion.169
  584.9 5.8 convolution_convert_fusion.1
  590.8 2.5 copy.57
  597.4 3.7 fusion.107
  601.1 6.3 reduce-scatter.10.cloned.1.call-done
  608.9 3.1 convolution_add_fusion.1
  612.0 21.1 %reduce-scatter.12.cloned.1.call-done = bf16[1,256,384]{1,2,0:T(8,128)(2,1)} async-done(((bf16[1,1024,384]{1,2,0:T(8,128)(2,1)}), bf16[1,256,384]{1,2,0:T(8,128)(2,1)}) %reduce-scatter.12.cloned.1.call-update) | async-done | bytes 196624 | tf_op jit(solution)/shard_map/reduce_scatter | solution.py:316
  633.1 3.3 fusion.47
  638.7 3.0 fusion.81
  641.8 4.5 fusion.87
  647.3 3.0 fusion.79
  650.6 7.6 fusion.108
  658.3 7.6 fusion.109
  667.1 7.7 fusion.71
  675.5 12.0 all-reduce.15.cloned.1.call-done
  689.2 61.8 %all-reduce.4 = (f32[1536]{0:T(1024)S(1)}, f32[1536]{0:T(1024)S(1)}) all-reduce(f32[1536]{0:T(1024)S(1)} %get-tuple-element.190, f32[1536]{0:T(1024)S(1)} %copy-done.35), channel_id=5, replica_groups=mesh['fsdp'=4,'ctx'=4,'tp'=2] {'fsdp','ctx'}, use_global_device_ids=true, to_apply=%region_18.19.clone | all-reduce | flops 3072 | bytes 24576
  752.1 3.3 fusion.68
  755.6 66.1 %reduce-scatter.18.cloned.1.call-done = f32[96,384]{1,0:T(8,128)} async-done(((f32[1536,384]{1,0:T(8,128)}), f32[96,384]{1,0:T(8,128)}) %reduce-scatter.18.cloned.1.call-update) | async-done | bytes 147472 | tf_op jit(solution)/shard_map/reduce_scatter | solution.py:355
  821.8 79.4 %reduce-scatter.20.cloned.1.call-done = f32[768,96]{0,1:T(8,128)} async-done(((f32[768,1536]{0,1:T(8,128)}), f32[768,96]{0,1:T(8,128)}) %reduce-scatter.20.cloned.1.call-update) | async-done | bytes 294928 | tf_op jit(solution)/shard_map/reduce_scatter | solution.py:356
  901.2 78.9 %reduce-scatter.14.cloned.1.call-done = f32[96,768]{1,0:T(8,128)} async-done(((f32[1536,768]{1,0:T(8,128)}), f32[96,768]{1,0:T(8,128)}) %reduce-scatter.14.cloned.1.call-update) | async-done | bytes 294928 | tf_op jit(solution)/shard_map/reduce_scatter | solution.py:353
  980.1 138.8 %reduce-scatter.22.cloned.1.call-done = f32[96,2048]{1,0:T(8,128)} async-done(((f32[1536,2048]{1,0:T(8,128)}), f32[96,2048]{1,0:T(8,128)}) %reduce-scatter.22.cloned.1.call-update) | async-done | bytes 786448 | tf_op jit(solution)/shard_map/reduce_scatter | solution.py:263
  1118.9 138.8 %reduce-scatter.24.cloned.1.call-done = f32[96,2048]{1,0:T(8,128)} async-done(((f32[1536,2048]{1,0:T(8,128)}), f32[96,2048]{1,0:T(8,128)}) %reduce-scatter.24.cloned.1.call-update) | async-done | bytes 786448 | tf_op jit(solution)/shard_map/reduce_scatter | solution.py:264
  1257.7 139.1 %reduce-scatter.26.cloned.1.call-done = f32[2048,96]{0,1:T(8,128)} async-done(((f32[2048,1536]{0,1:T(8,128)}), f32[2048,96]{0,1:T(8,128)}) %reduce-scatter.26.cloned.1.call-update) | async-done | bytes 786448 | tf_op jit(solution)/shard_map/reduce_scatter | solution.py:265
  (307 shorter events, 128.3 us)
Async XLA Ops:
  7.2 57.4 %copy-start = (bf16[1,256,1536]{2,1,0:T(8,128)(2,1)S(1)}, bf16[1,256,1536]{2,1,0:T(8,128)(2,1)}, u32[]{:S(2)}) copy-start(bf16[1,256,1536]{2,1,0:T(8,128)(2,1)} %param.17) | copy-start | bytes 2359300
  7.2 55.8 %all-gather.11.cloned.1.call-start = ((), (), s32[]{:S(2)}) async-start(), calls=%async_computation.10 | async-start | bytes 1253376 | tf_op jit(solution)/shard_map/all_gather | solution.py:150
  7.9 84.8 %all-gather.13.cloned.1.call-start = ((), (), s32[]{:S(2)}) async-start(), calls=%async_computation.11 | async-start | bytes 1253376 | tf_op jit(solution)/shard_map/all_gather | solution.py:151
  8.7 129.6 %all-gather.9.cloned.1.call-start = ((), (), s32[]{:S(2)}) async-start(), calls=%async_computation.9 | async-start | bytes 2506752 | tf_op jit(solution)/shard_map/all_gather | solution.py:149
  9.4 172.1 %all-gather.15.cloned.1.call-start = ((), (), s32[]{:S(2)}) async-start(), calls=%async_computation.12 | async-start | bytes 2506752 | tf_op jit(solution)/shard_map/all_gather | solution.py:152
  10.0 375.2 %all-reduce.11.cloned.1.call-start = ((), (), s32[]{:S(2)}) async-start(), calls=%async_computation.13 | async-start | bytes 3145728 | tf_op jit(solution)/shard_map/psum | solution.py:225
  52.8 88.3 %copy-start.33 = (f32[256]{0:T(256)}, f32[256]{0:T(256)S(1)}, u32[]{:S(2)}) copy-start(f32[256]{0:T(256)S(1)} %get-tuple-element.268) | copy-start | bytes 3076
  63.0 79.0 %copy-start.16 = (f32[256,48]{0,1:T(8,128)}, f32[256,48]{0,1:T(8,128)S(1)}, u32[]{:S(2)}) copy-start(f32[256,48]{0,1:T(8,128)S(1)} %get-tuple-element.265) | copy-start | bytes 147460
  63.0 79.0 %copy-start.18 = (f32[256,48]{0,1:T(8,128)}, f32[256,48]{0,1:T(8,128)S(1)}, u32[]{:S(2)}) copy-start(f32[256,48]{0,1:T(8,128)S(1)} %get-tuple-element.266) | copy-start | bytes 147460
  166.7 18.5 %copy-start.13 = (bf16[4,512,96]{2,1,0:T(8,128)(2,1)}, bf16[4,512,96]{2,1,0:T(8,128)(2,1)S(1)}, u32[]{:S(2)}) copy-start(bf16[4,512,96]{2,1,0:T(8,128)(2,1)S(1)} %get-tuple-element.531) | copy-start | bytes 1179652
  166.7 18.5 %copy-start.29 = (s32[4,1024]{1,0:T(4,128)}, s32[4,1024]{1,0:T(4,128)S(1)}, u32[]{:S(2)}) copy-start(s32[4,1024]{1,0:T(4,128)S(1)} %get-tuple-element.568) | copy-start | bytes 49156
  166.7 18.5 %copy-start.30 = (s32[256]{0:T(256)}, s32[256]{0:T(256)S(1)}, u32[]{:S(2)}) copy-start(s32[256]{0:T(256)S(1)} %get-tuple-element.574) | copy-start | bytes 3076
  166.7 18.5 %copy-start.32 = (s32[4,512]{1,0:T(4,128)}, s32[4,512]{1,0:T(4,128)S(1)}, u32[]{:S(2)}) copy-start(s32[4,512]{1,0:T(4,128)S(1)} %get-tuple-element.575) | copy-start | bytes 24580
  168.5 16.6 %copy-start.6 = (bf16[1,256,4,2,96]{1,4,3,2,0:T(8,128)(2,1)}, bf16[1,256,4,2,96]{1,4,3,2,0:T(8,128)(2,1)S(1)}, u32[]{:S(2)}) copy-start(bf16[1,256,4,2,96]{1,4,3,2,0:T(8,128)(2,1)S(1)} %copy.54) | copy-start | bytes 1179652
  185.2 202.0 %all-gather.17.cloned.1.call-start = ((), (), s32[]{:S(2)}) async-start(), calls=%async_computation.14 | async-start | bytes 6684672 | tf_op jit(solution)/shard_map/all_gather | solution.py:156
  185.8 224.1 %all-gather.19.cloned.1.call-start = ((), (), s32[]{:S(2)}) async-start(), calls=%async_computation.15 | async-start | bytes 6684672 | tf_op jit(solution)/shard_map/all_gather | solution.py:158
  186.5 286.4 %all-gather.21.cloned.1.call-start = ((), (), s32[]{:S(2)}) async-start(), calls=%async_computation.16 | async-start | bytes 6684672 | tf_op jit(solution)/shard_map/all_gather | solution.py:240
  186.6 13.7 collective-permute-start
  200.3 14.1 %collective-permute-start.1 = (bf16[96,2048]{1,0:T(8,128)(2,1)S(1)}, bf16[96,2048]{1,0:T(8,128)(2,1)S(1)}, u32[]{:S(2)}, u32[]{:S(2)}) collective-permute-start(bf16[96,2048]{1,0:T(8,128)(2,1)S(1)} %collective-permute-done), channel_id=1, source_target_pairs={{0,2},{2,4},{4,6},{6,8},{8,10},{10,12},{12,14},{14,16},{16,18},{18... | collective-permute-start | bytes 1179656 | tf_op jit(solution)/shard_map/ppermute | solution.py:31
  200.3 19.1 %collective-permute-start.8 = (bf16[96,2048]{1,0:T(8,128)(2,1)S(1)}, bf16[96,2048]{1,0:T(8,128)(2,1)S(1)}, u32[]{:S(2)}, u32[]{:S(2)}) collective-permute-start(bf16[96,2048]{1,0:T(8,128)(2,1)S(1)} %copy-done.14), channel_id=1, source_target_pairs={{2,0},{4,2},{6,4},{8,6},{10,8},{12,10},{14,12},{16,14},{18,16},{20... | collective-permute-start | bytes 1179656 | tf_op jit(solution)/shard_map/ppermute | solution.py:34
  214.4 16.9 %collective-permute-start.2 = (bf16[96,2048]{1,0:T(8,128)(2,1)S(1)}, bf16[96,2048]{1,0:T(8,128)(2,1)S(1)}, u32[]{:S(2)}, u32[]{:S(2)}) collective-permute-start(bf16[96,2048]{1,0:T(8,128)(2,1)S(1)} %collective-permute-done.1), channel_id=1, source_target_pairs={{0,2},{2,4},{4,6},{6,8},{8,10},{10,12},{12,14},{14,16},{16,18},{18... | collective-permute-start | bytes 1179656 | tf_op jit(solution)/shard_map/ppermute | solution.py:31
  219.4 18.2 %collective-permute-start.9 = (bf16[96,2048]{1,0:T(8,128)(2,1)S(1)}, bf16[96,2048]{1,0:T(8,128)(2,1)S(1)}, u32[]{:S(2)}, u32[]{:S(2)}) collective-permute-start(bf16[96,2048]{1,0:T(8,128)(2,1)S(1)} %collective-permute-done.8), channel_id=1, source_target_pairs={{2,0},{4,2},{6,4},{8,6},{10,8},{12,10},{14,12},{16,14},{18,16},{20... | collective-permute-start | bytes 1179656 | tf_op jit(solution)/shard_map/ppermute | solution.py:34
  231.3 16.9 %collective-permute-start.3 = (bf16[96,2048]{1,0:T(8,128)(2,1)S(1)}, bf16[96,2048]{1,0:T(8,128)(2,1)S(1)}, u32[]{:S(2)}, u32[]{:S(2)}) collective-permute-start(bf16[96,2048]{1,0:T(8,128)(2,1)S(1)} %collective-permute-done.2), channel_id=1, source_target_pairs={{0,2},{2,4},{4,6},{6,8},{8,10},{10,12},{12,14},{14,16},{16,18},{18... | collective-permute-start | bytes 1179656 | tf_op jit(solution)/shard_map/ppermute | solution.py:31
  237.6 36.8 %collective-permute-start.10 = (bf16[96,2048]{1,0:T(8,128)(2,1)S(1)}, bf16[96,2048]{1,0:T(8,128)(2,1)S(1)}, u32[]{:S(2)}, u32[]{:S(2)}) collective-permute-start(bf16[96,2048]{1,0:T(8,128)(2,1)S(1)} %collective-permute-done.9), channel_id=1, source_target_pairs={{2,0},{4,2},{6,4},{8,6},{10,8},{12,10},{14,12},{16,14},{18,16},{20... | collective-permute-start | bytes 1179656 | tf_op jit(solution)/shard_map/ppermute | solution.py:34
  248.2 50.9 %copy-start.25 = (bf16[96,2048]{1,0:T(8,128)(2,1)}, bf16[96,2048]{1,0:T(8,128)(2,1)S(1)}, u32[]{:S(2)}) copy-start(bf16[96,2048]{1,0:T(8,128)(2,1)S(1)} %collective-permute-done.3) | copy-start | bytes 1179652
  248.2 29.5 %collective-permute-start.4 = (bf16[96,2048]{1,0:T(8,128)(2,1)S(1)}, bf16[96,2048]{1,0:T(8,128)(2,1)S(1)}, u32[]{:S(2)}, u32[]{:S(2)}) collective-permute-start(bf16[96,2048]{1,0:T(8,128)(2,1)S(1)} %collective-permute-done.3), channel_id=1, source_target_pairs={{0,2},{2,4},{4,6},{6,8},{8,10},{10,12},{12,14},{14,16},{16,18},{18... | collective-permute-start | bytes 1179656 | tf_op jit(solution)/shard_map/ppermute | solution.py:31
  274.5 24.6 %collective-permute-start.11 = (bf16[96,2048]{1,0:T(8,128)(2,1)S(1)}, bf16[96,2048]{1,0:T(8,128)(2,1)S(1)}, u32[]{:S(2)}, u32[]{:S(2)}) collective-permute-start(bf16[96,2048]{1,0:T(8,128)(2,1)S(1)} %collective-permute-done.10), channel_id=1, source_target_pairs={{2,0},{4,2},{6,4},{8,6},{10,8},{12,10},{14,12},{16,14},{18,16},{20... | collective-permute-start | bytes 1179656 | tf_op jit(solution)/shard_map/ppermute | solution.py:34
  277.7 21.4 %copy-start.27 = (bf16[96,2048]{1,0:T(8,128)(2,1)}, bf16[96,2048]{1,0:T(8,128)(2,1)S(1)}, u32[]{:S(2)}) copy-start(bf16[96,2048]{1,0:T(8,128)(2,1)S(1)} %collective-permute-done.4) | copy-start | bytes 1179652
  277.7 26.6 %collective-permute-start.5 = (bf16[96,2048]{1,0:T(8,128)(2,1)S(1)}, bf16[96,2048]{1,0:T(8,128)(2,1)}, u32[]{:S(2)}, u32[]{:S(2)}) collective-permute-start(bf16[96,2048]{1,0:T(8,128)(2,1)S(1)} %collective-permute-done.4), channel_id=1, source_target_pairs={{0,2},{2,4},{4,6},{6,8},{8,10},{10,12},{12,14},{14,16},{16,18},{18... | collective-permute-start | bytes 1179656 | tf_op jit(solution)/shard_map/ppermute | solution.py:31
  299.1 65.6 %copy-start.23 = (bf16[96,2048]{1,0:T(8,128)(2,1)}, bf16[96,2048]{1,0:T(8,128)(2,1)S(1)}, u32[]{:S(2)}) copy-start(bf16[96,2048]{1,0:T(8,128)(2,1)S(1)} %collective-permute-done.11) | copy-start | bytes 1179652
  299.1 37.6 %collective-permute-start.12 = (bf16[96,2048]{1,0:T(8,128)(2,1)S(1)}, bf16[96,2048]{1,0:T(8,128)(2,1)}, u32[]{:S(2)}, u32[]{:S(2)}) collective-permute-start(bf16[96,2048]{1,0:T(8,128)(2,1)S(1)} %collective-permute-done.11), channel_id=1, source_target_pairs={{2,0},{4,2},{6,4},{8,6},{10,8},{12,10},{14,12},{16,14},{18,16},{20... | collective-permute-start | bytes 1179656 | tf_op jit(solution)/shard_map/ppermute | solution.py:34
  304.2 32.5 %collective-permute-start.6 = (bf16[96,2048]{1,0:T(8,128)(2,1)}, bf16[96,2048]{1,0:T(8,128)(2,1)}, u32[]{:S(2)}, u32[]{:S(2)}) collective-permute-start(bf16[96,2048]{1,0:T(8,128)(2,1)} %collective-permute-done.5), channel_id=1, source_target_pairs={{0,2},{2,4},{4,6},{6,8},{8,10},{10,12},{12,14},{14,16},{16,18},{18... | collective-permute-start | bytes 1179656 | tf_op jit(solution)/shard_map/ppermute | solution.py:31
  315.1 214.6 %all-reduce.13.cloned.1.call-start = ((), (), s32[]{:S(2)}) async-start(), calls=%async_computation.17 | async-start | bytes 3145728 | tf_op jit(solution)/shard_map/psum | solution.py:252
  336.7 19.1 %collective-permute-start.13 = (bf16[96,2048]{1,0:T(8,128)(2,1)}, bf16[96,2048]{1,0:T(8,128)(2,1)}, u32[]{:S(2)}, u32[]{:S(2)}) collective-permute-start(bf16[96,2048]{1,0:T(8,128)(2,1)} %collective-permute-done.12), channel_id=1, source_target_pairs={{2,0},{4,2},{6,4},{8,6},{10,8},{12,10},{14,12},{16,14},{18,16},{20... | collective-permute-start | bytes 1179656 | tf_op jit(solution)/shard_map/ppermute | solution.py:34
  336.7 24.4 %collective-permute-start.7 = (bf16[96,2048]{1,0:T(8,128)(2,1)}, bf16[96,2048]{1,0:T(8,128)(2,1)}, u32[]{:S(2)}, u32[]{:S(2)}) collective-permute-start(bf16[96,2048]{1,0:T(8,128)(2,1)} %collective-permute-done.6), channel_id=1, source_target_pairs={{0,2},{2,4},{4,6},{6,8},{8,10},{10,12},{12,14},{14,16},{16,18},{18... | collective-permute-start | bytes 1179656 | tf_op jit(solution)/shard_map/ppermute | solution.py:31
  339.5 27.0 %copy-start.28 = (bf16[96,2048]{1,0:T(8,128)(2,1)S(1)}, bf16[96,2048]{1,0:T(8,128)(2,1)}, u32[]{:S(2)}) copy-start(bf16[96,2048]{1,0:T(8,128)(2,1)} %copy-done.27) | copy-start | bytes 1179652
  339.5 27.8 %copy-start.26 = (bf16[96,2048]{1,0:T(8,128)(2,1)S(1)}, bf16[96,2048]{1,0:T(8,128)(2,1)}, u32[]{:S(2)}) copy-start(bf16[96,2048]{1,0:T(8,128)(2,1)} %copy-done.25) | copy-start | bytes 1179652
  355.9 22.1 %collective-permute-start.14 = (bf16[96,2048]{1,0:T(8,128)(2,1)}, bf16[96,2048]{1,0:T(8,128)(2,1)S(1)}, u32[]{:S(2)}, u32[]{:S(2)}) collective-permute-start(bf16[96,2048]{1,0:T(8,128)(2,1)} %collective-permute-done.13), channel_id=1, source_target_pairs={{2,0},{4,2},{6,4},{8,6},{10,8},{12,10},{14,12},{16,14},{18,16},{20... | collective-permute-start | bytes 1179656 | tf_op jit(solution)/shard_map/ppermute | solution.py:34
  366.5 3.9 copy-start.15
  369.6 3.9 copy-start.24
  409.9 5.0 copy-start.37
  409.9 12.8 slice-start
  414.9 7.8 slice-start.1
  479.5 127.9 %reduce-scatter.10.cloned.1.call-start = ((), (), s32[]{:S(2)}) async-start(), calls=%async_computation.18 | async-start | bytes 983040 | tf_op jit(solution)/shard_map/reduce_scatter | solution.py:310
  529.7 2.6 copy-start.5
  529.7 2.6 copy-start.10
  534.5 3.7 copy-start.31
  546.4 2.3 copy-start.22
  584.1 49.0 %reduce-scatter.12.cloned.1.call-start = ((), (), s32[]{:S(2)}) async-start(), calls=%async_computation.19 | async-start | bytes 983040 | tf_op jit(solution)/shard_map/reduce_scatter | solution.py:316
  584.9 102.6 %all-reduce.15.cloned.1.call-start = ((), (), s32[]{:S(2)}) async-start(), calls=%async_computation.27 | async-start | bytes 3145728 | tf_op jit(solution)/shard_map/psum | solution.py:233
  590.8 4.7 copy-start.17
  590.8 4.7 copy-start.19
  612.0 24.5 %copy-start.34 = (f32[256]{0:T(256)S(1)}, f32[256]{0:T(256)}, u32[]{:S(2)}) copy-start(f32[256]{0:T(256)} %copy-done.33) | copy-start | bytes 3076
  636.5 119.1 %reduce-scatter.16.cloned.1.call-start = ((), (), s32[]{:S(2)}) async-start(), calls=%async_computation.21 | async-start | bytes 2506752 | tf_op jit(solution)/shard_map/reduce_scatter | solution.py:354
  638.7 3.2 copy-start.7
  638.7 183.1 %reduce-scatter.18.cloned.1.call-start = ((), (), s32[]{:S(2)}) async-start(), calls=%async_computation.22 | async-start | bytes 2506752 | tf_op jit(solution)/shard_map/reduce_scatter | solution.py:355
  641.8 259.4 %reduce-scatter.20.cloned.1.call-start = ((), (), s32[]{:S(2)}) async-start(), calls=%async_computation.23 | async-start | bytes 5013504 | tf_op jit(solution)/shard_map/reduce_scatter | solution.py:356
  646.3 333.8 %reduce-scatter.14.cloned.1.call-start = ((), (), s32[]{:S(2)}) async-start(), calls=%async_computation.20 | async-start | bytes 5013504 | tf_op jit(solution)/shard_map/reduce_scatter | solution.py:353
  650.4 468.6 %reduce-scatter.22.cloned.1.call-start = ((), (), s32[]{:S(2)}) async-start(), calls=%async_computation.24 | async-start | bytes 13369344 | tf_op jit(solution)/shard_map/reduce_scatter | solution.py:263
  658.3 599.4 %reduce-scatter.24.cloned.1.call-start = ((), (), s32[]{:S(2)}) async-start(), calls=%async_computation.25 | async-start | bytes 13369344 | tf_op jit(solution)/shard_map/reduce_scatter | solution.py:264
  666.0 730.9 %reduce-scatter.26.cloned.1.call-start = ((), (), s32[]{:S(2)}) async-start(), calls=%async_computation.26 | async-start | bytes 13369344 | tf_op jit(solution)/shard_map/reduce_scatter | solution.py:265
  674.8 14.3 %copy-start.35 = (f32[1536]{0:T(1024)S(1)}, f32[1536]{0:T(1024)}, u32[]{:S(2)}) copy-start(f32[1536]{0:T(1024)} %get-tuple-element.188) | copy-start | bytes 18436
  674.8 77.2 %copy-start.36 = (f32[256]{0:T(256)S(1)}, f32[256]{0:T(256)}, u32[]{:S(2)}) copy-start(f32[256]{0:T(256)} %get-tuple-element.267) | copy-start | bytes 3076
  687.5 64.6 %copy-start.12 = (bf16[256,1536]{1,0:T(8,128)(2,1)S(1)}, bf16[256,1536]{1,0:T(8,128)(2,1)}, u32[]{:S(2)}) copy-start(bf16[256,1536]{1,0:T(8,128)(2,1)} %get-tuple-element.239) | copy-start | bytes 2359300
  (19 other events, 29.2 us)
Sparse Core Ops, SparseCore 0:
  10.3 41.4 all-gather.10
  54.1 38.5 all-gather.12
  95.1 43.1 all-gather.8
  140.4 41.0 all-gather.14
  185.3 50.2 all-reduce.10
  238.0 100.5 all-gather.16
  341.1 68.7 all-gather.18
  412.5 60.4 all-gather.20
  479.6 50.0 all-reduce.12
  584.3 23.1 reduce-scatter.9
  610.3 22.7 reduce-scatter.11
  636.6 50.8 all-reduce.14
  692.3 63.2 reduce-scatter.15
  759.8 61.9 reduce-scatter.17
  826.5 74.6 reduce-scatter.19
  905.5 74.5 reduce-scatter.13
  985.1 133.7 reduce-scatter.21
  1124.0 133.7 reduce-scatter.23
  1262.9 133.8 reduce-scatter.25
